TPU v7x, 32 devices: a whole 2x2x4 slice. The times are simulated.
32 devices in a mesh: grp: 4 (over y, x), seq: 8 (over z, core).
Axes of the slice: x: 2, y: 2, z: 4, core: 2. Of those that a mesh axis runs over, the one named last changes fastest.
Arguments:
- queries: bfloat16 [4096, 1024], P(('grp', 'seq')), may hold values from -6 to 6
- keys: bfloat16 [4096, 1024], P(('grp', 'seq')), may hold values from -11 to 11
- values: bfloat16 [4096, 1024], P(('grp', 'seq')), may hold values from -6 to 6
- forget: float32 [4096, 8], P(('grp', 'seq')), may hold values from 0 to 0.5
- beta: float32 [4096, 8], P(('grp', 'seq')), may hold values from 0 to 1
- level_weights: float32 [9, 4096, 8], P(None, ('grp', 'seq')), may hold values from 0.25 to 2
Outputs:
- output: float32 [4096, 1024], P(('grp', 'seq'))
All inputs are finite; a program needn't handle non-finite values.
Results may differ from a plain program's by a relative error of at most 0.0003.
Values sent between devices are 32-bit elements; how exact they have to be, the bound alone decides.
A program may use at most 64 MiB of HBM per device.

v0:
```python
import jax
import jax.numpy as jnp
from jax import lax
from jax.sharding import PartitionSpec as P

BLOCK = 128
LEVELS = 8


def partner(block, axis, distance):
    count = lax.axis_size(axis)
    route = []
    for low in range(count):
        high = low | 1 << distance
        if high != low and high < count:
            route += [(low, high), (high, low)]
    return lax.ppermute(block, axis, route)


def contract(form, left, right):
    return jnp.einsum(form, left, right, precision=lax.Precision.HIGHEST)


def unit_rows(array):
    return array * lax.rsqrt(jnp.sum(array * array, -1, keepdims=True) + 1e-06)


def block_step(carry, pieces):
    memory, transition = carry
    query_block, key_block, value_block, forget_block, beta_block = pieces
    length = query_block.shape[0]
    head_dim = query_block.shape[-1]
    query_heads = unit_rows(jnp.swapaxes(query_block.astype(jnp.float32), 0, 1))
    key_heads = unit_rows(jnp.swapaxes(key_block.astype(jnp.float32), 0, 1))
    value_heads = jnp.swapaxes(value_block.astype(jnp.float32), 0, 1)
    decays = jnp.exp(-jnp.cumsum(forget_block, 0)).T
    strength = beta_block.T
    strict = jnp.tril(jnp.ones((length, length), jnp.float32), -1)
    causal = jnp.tril(jnp.ones((length, length), jnp.float32), 0)
    intersections = contract("hsk,htk->hst", key_heads, key_heads)
    unit_lower = jnp.eye(length, dtype=jnp.float32) + strength[:, :, None] * intersections * strict
    right_sides = jnp.concatenate(
        [strength[:, :, None] * key_heads, (strength / decays)[:, :, None] * value_heads], -1
    )
    solved = lax.linalg.triangular_solve(
        unit_lower, right_sides, left_side=True, lower=True, unit_diagonal=True
    )
    update_rows = solved[..., :head_dim]
    write_rows = solved[..., head_dim:]
    scores = contract("htk,hsk->hts", query_heads, key_heads) * causal
    reached = decays[:, :, None] * (query_heads - contract("hts,hsk->htk", scores, update_rows))
    inside = decays[:, :, None] * contract("hts,hsv->htv", scores, write_rows) + contract(
        "hvk,htk->htv", memory, reached
    )
    reach_dev = contract("hkj,htj->htk", transition, reached)
    final_decay = decays[:, -1][:, None, None]
    step_trans = final_decay * (
        jnp.eye(head_dim, dtype=jnp.float32) - contract("hsk,hsj->hkj", update_rows, key_heads)
    )
    step_write = final_decay * contract("hsv,hsk->hvk", write_rows, key_heads)
    memory = contract("hvk,hkj->hvj", memory, step_trans) + step_write
    transition = contract("hik,hkj->hij", transition, step_trans)
    return ((memory, transition), (inside, reach_dev))


def compose(lower_trans, lower_state, upper_trans, upper_state):
    joined_trans = contract("...ik,...kj->...ij", lower_trans, upper_trans)
    joined_state = contract("...vk,...kj->...vj", lower_state, upper_trans) + upper_state
    return (joined_trans, joined_state)


def pair_round(block_trans, block_state, peer_trans, peer_state, is_upper, prior_trans):
    level = jnp.where(is_upper, contract("hvk,hkj->hvj", peer_state, prior_trans), 0.0)
    lower_trans = jnp.where(is_upper, peer_trans, block_trans)
    lower_state = jnp.where(is_upper, peer_state, block_state)
    upper_trans = jnp.where(is_upper, block_trans, peer_trans)
    upper_state = jnp.where(is_upper, block_state, peer_state)
    block_trans, block_state = compose(lower_trans, lower_state, upper_trans, upper_state)
    prior_trans = jnp.where(
        is_upper, contract("hik,hkj->hij", peer_trans, prior_trans), prior_trans
    )
    return (block_trans, block_state, prior_trans, level)


def on_device(queries, keys, values, forget, beta, level_weights):
    tokens = queries.shape[0]
    heads = forget.shape[1]
    head_dim = queries.shape[1] // heads
    blocks = tokens // BLOCK

    def into_blocks(array):
        return array.reshape((blocks, BLOCK) + array.shape[1:])

    shaped = (tokens, heads, head_dim)
    pieces = (
        into_blocks(queries.reshape(shaped)),
        into_blocks(keys.reshape(shaped)),
        into_blocks(values.reshape(shaped)),
        into_blocks(forget),
        into_blocks(beta),
    )
    identity = jnp.broadcast_to(jnp.eye(head_dim, dtype=jnp.float32), (heads, head_dim, head_dim))
    start = (jnp.zeros((heads, head_dim, head_dim), jnp.float32), identity)
    (memory, transition), (inside, reached) = lax.scan(block_step, start, pieces)
    inside = jnp.swapaxes(inside, 0, 1).reshape(heads, tokens, head_dim)
    reached = jnp.swapaxes(reached, 0, 1).reshape(heads, tokens, head_dim)
    levels = []
    prior_trans = identity
    block_trans, block_state = (transition, memory)
    position = lax.axis_index(("grp", "seq"))
    for level_bit in range(lax.axis_size(("grp", "seq")).bit_length() - 1):
        peer_trans, peer_state = partner((block_trans, block_state), ("grp", "seq"), level_bit)
        is_upper = position >> level_bit & 1 == 1
        block_trans, block_state, prior_trans, level = pair_round(
            block_trans, block_state, peer_trans, peer_state, is_upper, prior_trans
        )
        levels.append(level)
    while len(levels) < LEVELS:
        levels.append(jnp.zeros((heads, head_dim, head_dim), jnp.float32))
    stacked = jnp.stack(levels, 1)
    level_mats = jnp.swapaxes(stacked, 2, 3).reshape(heads, LEVELS * head_dim, head_dim)
    weights_heads = jnp.transpose(level_weights[1:], (2, 1, 0))

    def per_head(entry):
        reach_head, weight_head, matrix_head = entry
        scaled = (weight_head[:, :, None] * reach_head[:, None, :]).reshape(
            tokens, LEVELS * head_dim
        )
        return jnp.dot(
            scaled, matrix_head, precision=lax.Precision.HIGHEST, preferred_element_type=jnp.float32
        )

    far_part = lax.map(per_head, (reached, weights_heads, level_mats))
    result = level_weights[0].T[:, :, None] * inside + far_part
    return jnp.swapaxes(result, 0, 1).reshape(tokens, heads * head_dim)


def solution(mesh):
    return jax.shard_map(
        on_device,
        mesh=mesh,
        in_specs=(
            P(("grp", "seq"), None),
            P(("grp", "seq"), None),
            P(("grp", "seq"), None),
            P(("grp", "seq"), None),
            P(("grp", "seq"), None),
            P(None, ("grp", "seq"), None),
        ),
        out_specs=P(("grp", "seq"), None),
        check_vma=False,
    )
```

profile of v0, /device:TPU:0, one launch (start us, length us, event | category | flops | bytes accessed | tf_op | source)
XLA Modules:
  0.0 231.1 jit_solution(9655336136311693517)
XLA Ops:
  6.8 79.2 %custom-call.4 = f32[8,1,128,128]{2,3,1,0:T(8,128)} custom-call(f32[8,1,128,128]{3,2,1,0:T(8,128)S(1)} %fusion.20), custom_call_target="InvertDiagBlocksLowerTriangular" | custom-call | tf_op jit(solution)/shard_map/while/body/eval_jaxpr/triangular_solve | solution.py:45
  86.2 2.1 fusion.21
  90.1 2.0 fusion.11
  95.6 1.8 fusion.51
  97.5 2.0 convolution_multiply_fusion.1
  99.5 1.6 fusion.6
  102.9 3.1 %collective-permute-start.3 = (f32[8,128,128]{2,1,0:T(8,128)S(1)}, f32[8,128,128]{2,1,0:T(8,128)S(1)}, u32[]{:S(2)}, u32[]{:S(2)}) collective-permute-start(f32[8,128,128]{2,1,0:T(8,128)S(1)} %fusion.34), channel_id=1, source_target_pairs={{0,2},{2,0},{1,3},{3,1},{4,6},{6,4},{5,7},{7,5},{8,10},{10,8},{9,1... | collective-permute-start | bytes 1572872 | tf_op jit(solution)/shard_map/ppermute | solution.py:17
  106.0 2.0 convolution_add_fusion.3
  109.9 8.9 %collective-permute-done.3 = f32[8,128,128]{2,1,0:T(8,128)S(1)} collective-permute-done((f32[8,128,128]{2,1,0:T(8,128)S(1)}, f32[8,128,128]{2,1,0:T(8,128)S(1)}, u32[]{:S(2)}, u32[]{:S(2)}) %collective-permute-start.3) | collective-permute-done | bytes 524320 | tf_op jit(solution)/shard_map/ppermute | solution.py:17
  119.5 3.1 %collective-permute-start.5 = (f32[8,128,128]{2,1,0:T(8,128)S(1)}, f32[8,128,128]{2,1,0:T(8,128)S(1)}, u32[]{:S(2)}, u32[]{:S(2)}) collective-permute-start(f32[8,128,128]{2,1,0:T(8,128)S(1)} %fusion.31), channel_id=1, source_target_pairs={{0,4},{4,0},{1,5},{5,1},{2,6},{6,2},{3,7},{7,3},{8,12},{12,8},{9,1... | collective-permute-start | bytes 1572872 | tf_op jit(solution)/shard_map/ppermute | solution.py:17
  122.6 16.6 %collective-permute-done.2 = f32[8,128,128]{2,1,0:T(8,128)S(1)} collective-permute-done((f32[8,128,128]{2,1,0:T(8,128)S(1)}, f32[8,128,128]{2,1,0:T(8,128)S(1)}, u32[]{:S(2)}, u32[]{:S(2)}) %collective-permute-start.2) | collective-permute-done | bytes 524320 | tf_op jit(solution)/shard_map/ppermute | solution.py:17
  139.2 1.5 convolution_add_fusion.2
  140.6 1.5 fusion.7
  145.7 1.8 collective-permute-start.7
  147.5 20.5 %collective-permute-done.4 = f32[8,128,128]{2,1,0:T(8,128)S(1)} collective-permute-done((f32[8,128,128]{2,1,0:T(8,128)}, f32[8,128,128]{2,1,0:T(8,128)S(1)}, u32[]{:S(2)}, u32[]{:S(2)}) %collective-permute-start.4) | collective-permute-done | bytes 524320 | tf_op jit(solution)/shard_map/ppermute | solution.py:17
  168.0 1.5 convolution_add_fusion.1
  169.5 1.5 collective-permute-start.6
  173.4 10.3 %collective-permute-done.6 = f32[8,128,128]{2,1,0:T(8,128)} collective-permute-done((f32[8,128,128]{2,1,0:T(8,128)}, f32[8,128,128]{2,1,0:T(8,128)}, u32[]{:S(2)}, u32[]{:S(2)}) %collective-permute-start.6) | collective-permute-done | bytes 524320 | tf_op jit(solution)/shard_map/ppermute | solution.py:17
  183.7 3.0 %convolution_add_fusion = f32[8,128,128]{2,1,0:T(8,128)} fusion(f32[8,128,128]{2,1,0:T(8,128)} %convolution_add_fusion.1, f32[8,128,128]{2,1,0:T(8,128)} %collective-permute-done.6, f32[8,128,128]{2,1,0:T(8,128)S(1)} %fusion.28, f32[8,128,128]{2,1,0:T(8,128)} %collective-permute-done.7, pred[]{:T(512)S(6)} %eq.41), kind=kOutput, calls=%fused_computation.24 | convolution fusion | flops 201850880 | bytes 2621441 | tf_op jit(solution)/shard_map/...vk,...kj->...vj/dot_general | solution.py:21
  186.7 1.5 collective-permute-start.8
  188.2 1.7 fusion.9
  191.0 1.7 convolution_select_fusion
  192.7 7.2 %collective-permute-done.8 = f32[8,128,128]{2,1,0:T(8,128)S(1)} collective-permute-done((f32[8,128,128]{2,1,0:T(8,128)}, f32[8,128,128]{2,1,0:T(8,128)S(1)}, u32[]{:S(2)}, u32[]{:S(2)}) %collective-permute-start.8) | collective-permute-done | bytes 524320 | tf_op jit(solution)/shard_map/ppermute | solution.py:17
  203.5 25.9 %while.2 = (s32[]{:T(128)}, f32[8,128,128]{1,2,0:T(8,128)S(1)}, f32[8,128,8]{1,2,0:T(8,128)S(1)}, f32[8,128,128]{2,1,0:T(8,128)}, f32[8,1024,128]{2,1,0:T(8,128)}, /*index=5*/s32[]{:T(128)}) while((s32[]{:T(128)}, f32[8,128,128]{1,2,0:T(8,128)S(1)}, f32[8,128,8]{1,2,0:T(8,128)S(1)}, f32[8,128,128]{2,1,0:T(8,128)}, f32[8,1024,128]{2,1,0:T(8,128)}, ...), condition=%wide.region_4.5_spmd, body=%wide.region_3.4_spmd.sunk | while | flops 201457664 | bytes 1856597 | solution.py:133
  204.8 2.0 fusion.98
  208.0 2.0 fusion.98
  211.2 2.0 fusion.98
  214.4 2.0 fusion.98
  217.7 2.0 fusion.98
  220.9 2.0 fusion.98
  224.1 2.0 fusion.98
  227.4 2.0 fusion.98
  (114 shorter events, 37.8 us)
Async XLA Ops:
  0.0 5.1 %copy-start.8 = (f32[128,8]{0,1:T(8,128)S(1)}, f32[128,8]{0,1:T(8,128)}, u32[]{:S(2)}) copy-start(f32[128,8]{0,1:T(8,128)} %param.12) | copy-start | bytes 12292
  0.0 4.9 %copy-start.6 = (bf16[128,1024]{1,0:T(8,128)(2,1)S(1)}, bf16[128,1024]{1,0:T(8,128)(2,1)}, u32[]{:S(2)}) copy-start(bf16[128,1024]{1,0:T(8,128)(2,1)} %param.8) | copy-start | bytes 786436
  90.1 7.4 %slice-start = ((f32[9,128,8]{1,2,0:T(8,128)}), f32[8,128,8]{1,2,0:T(8,128)S(1)}, s32[]{:S(2)}) async-start(f32[9,128,8]{1,2,0:T(8,128)} %param.13), calls=%async_computation | async-start | bytes 65536 | tf_op jit(solution)/shard_map/slice | solution.py:122
  90.1 7.4 %copy-start.7 = (f32[9,128,8]{1,2,0:T(8,128)S(1)}, f32[9,128,8]{1,2,0:T(8,128)}, u32[]{:S(2)}) copy-start(f32[9,128,8]{1,2,0:T(8,128)} %param.13) | copy-start | bytes 110596
  92.1 7.4 %collective-permute-start = (f32[8,128,128]{2,1,0:T(8,128)}, f32[8,128,128]{2,1,0:T(8,128)}, u32[]{:S(2)}, u32[]{:S(2)}) collective-permute-start(f32[8,128,128]{2,1,0:T(8,128)} %fusion.11), channel_id=1, source_target_pairs={{0,1},{1,0},{2,3},{3,2},{4,5},{5,4},{6,7},{7,6},{8,9},{9,8},{10,11... | collective-permute-start | bytes 1572872 | tf_op jit(solution)/shard_map/ppermute | solution.py:17
  93.2 9.0 %collective-permute-start.1 = (f32[8,128,128]{2,1,0:T(8,128)S(1)}, f32[8,128,128]{2,1,0:T(8,128)S(1)}, u32[]{:S(2)}, u32[]{:S(2)}) collective-permute-start(f32[8,128,128]{2,1,0:T(8,128)S(1)} %fusion.48), channel_id=1, source_target_pairs={{0,1},{1,0},{2,3},{3,2},{4,5},{5,4},{6,7},{7,6},{8,9},{9,8},{10,11... | collective-permute-start | bytes 1572872 | tf_op jit(solution)/shard_map/ppermute | solution.py:17
  94.6 1.0 copy-start
  95.6 12.4 %copy-start.1 = (f32[8,128,128]{1,2,0:T(8,128)}, f32[8,128,128]{1,2,0:T(8,128)S(1)}, u32[]{:S(2)}) copy-start(f32[8,128,128]{1,2,0:T(8,128)S(1)} %fusion.15) | copy-start | bytes 1572868
  102.2 5.9 %copy-start.3 = (f32[8,1,128,128]{2,3,1,0:T(8,128)S(1)}, f32[8,1,128,128]{2,3,1,0:T(8,128)}, u32[]{:S(2)}) copy-start(f32[8,1,128,128]{2,3,1,0:T(8,128)} %copy.69) | copy-start | bytes 1572868
  102.9 15.9 %collective-permute-start.3 = (f32[8,128,128]{2,1,0:T(8,128)S(1)}, f32[8,128,128]{2,1,0:T(8,128)S(1)}, u32[]{:S(2)}, u32[]{:S(2)}) collective-permute-start(f32[8,128,128]{2,1,0:T(8,128)S(1)} %fusion.34), channel_id=1, source_target_pairs={{0,2},{2,0},{1,3},{3,1},{4,6},{6,4},{5,7},{7,5},{8,10},{10,8},{9,1... | collective-permute-start | bytes 1572872 | tf_op jit(solution)/shard_map/ppermute | solution.py:17
  108.1 31.1 %collective-permute-start.2 = (f32[8,128,128]{2,1,0:T(8,128)S(1)}, f32[8,128,128]{2,1,0:T(8,128)S(1)}, u32[]{:S(2)}, u32[]{:S(2)}) collective-permute-start(f32[8,128,128]{2,1,0:T(8,128)S(1)} %convolution_add_fusion.3), channel_id=1, source_target_pairs={{0,2},{2,0},{1,3},{3,1},{4,6},{6,4},{5,7},{7,5},{8,10},{10,8},{9,1... | collective-permute-start | bytes 1572872 | tf_op jit(solution)/shard_map/ppermute | solution.py:17
  119.5 25.5 %collective-permute-start.5 = (f32[8,128,128]{2,1,0:T(8,128)S(1)}, f32[8,128,128]{2,1,0:T(8,128)S(1)}, u32[]{:S(2)}, u32[]{:S(2)}) collective-permute-start(f32[8,128,128]{2,1,0:T(8,128)S(1)} %fusion.31), channel_id=1, source_target_pairs={{0,4},{4,0},{1,5},{5,1},{2,6},{6,2},{3,7},{7,3},{8,12},{12,8},{9,1... | collective-permute-start | bytes 1572872 | tf_op jit(solution)/shard_map/ppermute | solution.py:17
  143.4 24.7 %copy-start.4 = (f32[8,128,128]{2,1,0:T(8,128)S(1)}, f32[8,128,128]{2,1,0:T(8,128)}, u32[]{:S(2)}) copy-start(f32[8,128,128]{2,1,0:T(8,128)} %convolution_add_fusion.2) | copy-start | bytes 1572868
  143.4 24.7 %collective-permute-start.4 = (f32[8,128,128]{2,1,0:T(8,128)}, f32[8,128,128]{2,1,0:T(8,128)S(1)}, u32[]{:S(2)}, u32[]{:S(2)}) collective-permute-start(f32[8,128,128]{2,1,0:T(8,128)} %convolution_add_fusion.2), channel_id=1, source_target_pairs={{0,4},{4,0},{1,5},{5,1},{2,6},{6,2},{3,7},{7,3},{8,12},{12,8},{9,1... | collective-permute-start | bytes 1572872 | tf_op jit(solution)/shard_map/ppermute | solution.py:17
  145.7 27.7 %collective-permute-start.7 = (f32[8,128,128]{2,1,0:T(8,128)S(1)}, f32[8,128,128]{2,1,0:T(8,128)}, u32[]{:S(2)}, u32[]{:S(2)}) collective-permute-start(f32[8,128,128]{2,1,0:T(8,128)S(1)} %fusion.28), channel_id=1, source_target_pairs={{0,8},{8,0},{1,9},{9,1},{2,10},{10,2},{3,11},{11,3},{4,12},{12,4},... | collective-permute-start | bytes 1572872 | tf_op jit(solution)/shard_map/ppermute | solution.py:17
  169.5 14.2 %collective-permute-start.6 = (f32[8,128,128]{2,1,0:T(8,128)}, f32[8,128,128]{2,1,0:T(8,128)}, u32[]{:S(2)}, u32[]{:S(2)}) collective-permute-start(f32[8,128,128]{2,1,0:T(8,128)} %convolution_add_fusion.1), channel_id=1, source_target_pairs={{0,8},{8,0},{1,9},{9,1},{2,10},{10,2},{3,11},{11,3},{4,12},{12,4},... | collective-permute-start | bytes 1572872 | tf_op jit(solution)/shard_map/ppermute | solution.py:17
  186.7 13.2 %collective-permute-start.8 = (f32[8,128,128]{2,1,0:T(8,128)}, f32[8,128,128]{2,1,0:T(8,128)S(1)}, u32[]{:S(2)}, u32[]{:S(2)}) collective-permute-start(f32[8,128,128]{2,1,0:T(8,128)} %convolution_add_fusion), channel_id=1, source_target_pairs={{0,16},{16,0},{1,17},{17,1},{2,18},{18,2},{3,19},{19,3},{4,20},{20... | collective-permute-start | bytes 1572872 | tf_op jit(solution)/shard_map/ppermute | solution.py:17
  190.1 13.4 %copy-start.5 = (f32[8,128,128]{1,2,0:T(8,128)S(1)}, f32[8,128,128]{1,2,0:T(8,128)}, u32[]{:S(2)}) copy-start(f32[8,128,128]{1,2,0:T(8,128)} %custom-call.6) | copy-start | bytes 1572868
  203.5 25.9 %copy-start.2 = (f32[8,128,128]{1,2,0:T(8,128)S(1)}, f32[8,128,128]{1,2,0:T(8,128)}, u32[]{:S(2)}) copy-start(f32[8,128,128]{1,2,0:T(8,128)} %copy-done.1) | copy-start | bytes 1572868
where the time goes:
time: 232 us; the launch traced here: 231 us
  other arithmetic  82 us (35%)
  waiting for transfers between devices  63.6 us (27%)
  matrix products  50.8 us (22%)
  local copies, waits for them, and re-layouts  22.2 us (10%)
  starting transfers between devices  11.8 us (5%)
    another operation x5, other arithmetic, block_step(): lax.linalg.triangular_solve(unit_lower, right_sides, left_side=True, lowe...  79.3 us
    ppermute x9, waiting for transfers between devices, partner(): return lax.ppermute(block, axis, route)  63.6 us
    dot_general x26, matrix products, contract(): return jnp.einsum(form, left, right, precision=lax.Precision.HIGHEST)  32.3 us
    dot_general x8, matrix products, per_head(): jnp.dot(scaled, matrix_head, precision=lax.Precision.HIGHEST, preferred_e...  16.4 us
    ppermute x9, starting transfers between devices, partner(): return lax.ppermute(block, axis, route)  11.8 us
    unnamed x29, local copies, waits for them, and re-layouts  9.05 us
    mul x24, local copies, waits for them, and re-layouts, per_head(): weight_head[:, :, None] * reach_head[:, None, :]  7.67 us
  transfers between devices with their start and end apart: 9, of which 5 were waited for; matrix products, arithmetic and copies ran while one was open for 12% of the time, Pallas kernels for 0%

commit v1 on v0

v1 whole, which is shorter than its diff:
```python
import functools

import jax
import jax.numpy as jnp
from jax import lax
from jax.experimental import pallas as pl
from jax.experimental.pallas import tpu as pltpu
from jax.sharding import PartitionSpec as P

MESH = pl.DeviceIdType.MESH
F32 = jnp.float32
BF16 = jnp.bfloat16
NN = (((1,), (0,)), ((), ()))
NT = (((1,), (1,)), ((), ()))
AUX = 16


def group_bits(heads, n_seq):
    need = heads.bit_length() - 1
    return tuple(range(need - 1)) + (n_seq.bit_length() - 1,)


def dot(a, b, dims=NN):
    return lax.dot_general(a, b, dims, preferred_element_type=F32)


def split(a):
    high = a.astype(BF16)
    return high, (a - high.astype(F32)).astype(BF16)


def mm(a, b, dims=NN):
    ah, al = a
    bh, bl = b
    return dot(ah, bh, dims) + (dot(ah, bl, dims) + dot(al, bh, dims))


def mm_exact(a, b):
    high, low = split(a)
    return dot(high, b) + dot(low, b)


def unit_lower_inverse(lowers, size, row, col):
    apart = row ^ col
    eye = (apart == 0).astype(F32)
    inverses = [eye - jnp.where(apart == 1, low, 0.0) for low in lowers]
    width = 2
    while width < size:
        mask = (apart >= width) & (apart < 2 * width)
        parts = [split(x) for x in inverses]
        blocks = [split(jnp.where(mask, low, 0.0)) for low in lowers]
        left = [split(mm(x, b)) for x, b in zip(parts, blocks)]
        inverses = [x - mm(l, p) for x, l, p in zip(inverses, left, parts)]
        width *= 2
    return inverses


def transitions(blocks, size, dim):
    row = lax.broadcasted_iota(jnp.int32, (size, size), 0)
    col = lax.broadcasted_iota(jnp.int32, (size, size), 1)
    staged = []
    lowers = []
    for block in blocks:
        k, v, aux = block[:size], block[size : 2 * size], block[2 * size :]
        cols = aux.T
        rk = lax.rsqrt(jnp.sum(k * k, -1, keepdims=True) + 1e-06)
        rk_row = jnp.broadcast_to(rk, (size, size)).T
        kb, vb = k.astype(BF16), v.astype(BF16)
        lowers.append(jnp.where(row > col, dot(kb, kb, NT) * rk * rk_row * cols[:, 1:2], 0.0))
        staged.append((kb, vb, rk, rk_row, aux[0:1], aux[1:2], cols))
    inverses = unit_lower_inverse(lowers, size, row, col)
    results = []
    eye = (row == col).astype(F32)
    for inverse, (kb, vb, rk, rk_row, decay_row, beta_row, cols) in zip(inverses, staged):
        update = mm_exact(inverse * (rk_row * beta_row), kb)
        write = mm_exact(inverse * (beta_row / decay_row), vb)
        pair = jnp.concatenate([update, write], 1)
        last = decay_row[:, size - 1 : size]
        moved = mm_exact((pair * rk).T, kb)
        node = jnp.concatenate([last * (eye - moved[:dim]), last * moved[dim:]], 0)
        results.append((node, pair, cols, rk_row))
    return results


def local_reads(q, kb, pair, cols, rk_row, dim):
    size = q.shape[0]
    row = lax.broadcasted_iota(jnp.int32, (size, size), 0)
    col = lax.broadcasted_iota(jnp.int32, (size, size), 1)
    rq = lax.rsqrt(jnp.sum(q * q, -1, keepdims=True) + 1e-06)
    scores = jnp.where(row >= col, dot(q.astype(BF16), kb, NT) * rq * rk_row, 0.0)
    seen = mm(split(scores), split(pair))
    decay_col = cols[:, 0:1]
    return decay_col * (q * rq - seen[:, :dim]), decay_col * seen[:, dim:] * cols[:, 2:3]


def join(lower, upper, dim):
    both = mm(split(lower), split(upper[:dim]))
    return jnp.concatenate([both[:dim], both[dim:] + upper[dim:]], 0)


def kernel(n_grp, n_seq, heads, *refs):
    q_ref, k_ref, v_ref, aux_ref, out_ref = refs[:5]
    kv_out, q_out, kv_in, q_in, pairs, cols, rks, reach, acc, joined = refs[5:15]
    bits = group_bits(heads, n_seq)
    low_levels = len(bits) - 1
    cross = bits[-1]
    total_bits = (n_grp * n_seq).bit_length() - 1
    middle = list(range(low_levels, cross))
    upward = list(range(cross + 1, total_bits))
    refs = refs[15:]
    trees, refs = refs[:low_levels], refs[low_levels:]
    n_mid, n_up = len(middle), len(upward)
    mid_out, mid_in = refs[:n_mid], refs[n_mid : 2 * n_mid]
    refs = refs[2 * n_mid :]
    up_out, up_in = refs[:n_up], refs[n_up : 2 * n_up]
    s_kv, r_kv, s_q, r_q, s_mid, r_mid, s_up, r_up, s_out, r_out = refs[2 * n_up :]
    size = q_ref.shape[0]
    dim = q_ref.shape[1] // heads
    half = heads // 2
    pos = lax.axis_index("grp") * n_seq + lax.axis_index("seq")

    def bit_of(number, l):
        return (number // (1 << l)) % 2

    me = sum(bit_of(pos, l) * (1 << m) for m, l in enumerate(bits))
    base = pos - sum(bit_of(pos, l) * (1 << l) for l in bits)
    side, place = me // half, me % half

    def where_is(number):
        return (number // n_seq, number % n_seq)

    def member(i):
        return where_is(base + sum(bit_of(i, m) * (1 << l) for m, l in enumerate(bits)))

    def partner(l):
        return where_is(pos + (1 - 2 * bit_of(pos, l)) * (1 << l))

    def slot(rank, sign):
        far, r = rank // half, rank % half
        spot = (place + half + sign * 2 * (r // 2)) % half
        if r % 2:
            spot = spot + 1 - 2 * (spot % 2)
        which = 1 - side if far else side
        return which * half + spot

    def columns(i):
        return pl.ds(pl.multiple_of(i * dim, dim), dim)

    barrier = pltpu.get_barrier_semaphore()
    for rank in range(1, heads):
        pl.semaphore_signal(
            barrier, inc=1, device_id=member(slot(rank, 1)), device_id_type=MESH
        )
    for l in middle + upward:
        pl.semaphore_signal(barrier, inc=1, device_id=partner(l), device_id_type=MESH)
    for i in range(heads):
        part = slice(i * dim, (i + 1) * dim)
        kv_out[i, :size] = k_ref[:, part].astype(F32)
        kv_out[i, size : 2 * size] = v_ref[:, part].astype(F32)
        kv_out[i, 2 * size :] = aux_ref[i]
        q_out[i] = q_ref[:, part].astype(F32)
    pl.semaphore_wait(barrier, heads - 1 + n_mid + n_up)

    def remote(source, target, send, receive, device):
        copy = pltpu.make_async_remote_copy(
            src_ref=source,
            dst_ref=target,
            send_sem=send,
            recv_sem=receive,
            device_id=device,
            device_id_type=MESH,
        )
        return copy

    pending = []
    kv_copies, q_copies = [], []
    for out, into, send, receive, copies in (
        (kv_out, kv_in, s_kv, r_kv, kv_copies),
        (q_out, q_in, s_q, r_q, q_copies),
    ):
        for rank in range(1, heads):
            i = slot(rank, 1)
            copy = remote(out.at[i], into.at[me], send.at[rank], receive.at[rank], member(i))
            copy.start()
            copies.append(copy)
    pending += kv_copies + q_copies
    kv_in[me] = kv_out[me]
    q_in[me] = q_out[me]

    mid_copies = [{} for l in middle]

    def send_mid(m, which):
        copy = remote(
            mid_out[m].at[which],
            mid_in[m].at[which],
            s_mid.at[m, which],
            r_mid.at[m, which],
            partner(middle[m]),
        )
        copy.start()
        pending.append(copy)
        return copy

    first_mid = []
    for far in range(2):
        which = 1 - side if far else side
        for first in range(0, half, 2):
            slots = []
            for rank in (far * half + first, far * half + first + 1):
                if rank:
                    kv_copies[rank - 1].wait_recv()
                slots.append(slot(rank, -1))
            done = transitions([kv_in[i] for i in slots], size, dim)
            for i, (node, pair, col, rk_row) in zip(slots, done):
                trees[0][i] = node
                pairs[i] = pair
                cols[i] = col
                rks[i] = rk_row[:8]
        for m in range(low_levels):
            count = half >> (m + 1)
            for j in range(count):
                lower = trees[m][which * 2 * count + 2 * j]
                upper = trees[m][which * 2 * count + 2 * j + 1]
                node = join(lower, upper, dim)
                if m + 1 < low_levels:
                    trees[m + 1][which * count + j] = node
                else:
                    mid_out[0][which] = node
        first_mid.append(send_mid(0, which))

    def read(j, lower, l, gate=None):
        seen = mm(split(reach[j]), lower, NT)
        far = cols[j, :, 3 + l : 4 + l] * seen[:, seen.shape[1] - dim :]
        acc[j] += far if gate is None else jnp.where(gate, far, 0.0)
        if seen.shape[1] > dim:
            new = seen[:, :dim]
            reach[j] = new if gate is None else jnp.where(gate, new, reach[j])

    for first in range(0, heads, 2):
        for rank in (first, first + 1):
            if rank:
                q_copies[rank - 1].wait_recv()
            i = slot(rank, -1)
            rk_row = jnp.broadcast_to(rks[i][:1], (size, size))
            near = local_reads(
                q_in[i], kv_in[i, :size, :].astype(BF16), pairs[i], cols[i], rk_row, dim
            )
            reach[i], acc[i] = near
    for m in range(low_levels):
        for key in range(0, heads, 2 << m):
            lower = split(trees[m][key >> m])
            for j in range(key + (1 << m), key + (2 << m)):
                read(j, lower, m)

    copies = first_mid
    for m, l in enumerate(middle):
        upper_side = bit_of(pos, l) == 1
        following = []
        for far in range(2):
            which = 1 - side if far else side
            copies[far].wait_recv()
            peer, mine = mid_in[m][which], mid_out[m][which]
            lower = jnp.where(upper_side, peer, mine)
            upper = jnp.where(upper_side, mine, peer)
            node = join(lower, upper, dim)
            if m + 1 < n_mid:
                mid_out[m + 1][which] = node
                following.append(send_mid(m + 1, which))
            else:
                joined[which] = node
        copies = following

    node = join(joined[0], joined[1], dim)

    def send_up(m):
        copy = remote(up_out[m], up_in[m], s_up.at[m], r_up.at[m], partner(upward[m]))
        copy.start()
        pending.append(copy)
        return copy

    up_out[0][...] = node[dim:] if n_up == 1 else node
    copy = send_up(0)
    for m, l in enumerate(middle):
        gate = bit_of(pos, l) == 1
        for which in range(2):
            lower = split(mid_in[m][which])
            for j in range(which * half, (which + 1) * half):
                read(j, lower, l, gate)
    lower = split(joined[0])
    for j in range(half, heads):
        read(j, lower, cross)
    for m, l in enumerate(upward):
        gate = bit_of(pos, l) == 1
        copy.wait_recv()
        peer = up_in[m][...]
        if m + 1 < n_up:
            mine = up_out[m][...]
            node = join(jnp.where(gate, peer, mine), jnp.where(gate, mine, peer), dim)
            up_out[m + 1][...] = node[dim:] if m + 2 == n_up else node
            copy = send_up(m + 1)
        lower = split(peer)
        for rank in range(heads - 1, -1, -1):
            if m + 1 < n_up:
                read(rank, lower, l, gate)
                continue
            i = slot(rank, 1)
            read(i, lower, l, gate)
            if rank == 0:
                out_ref[:, columns(me)] = acc[me]
                continue
            back = remote(
                acc.at[i], out_ref.at[:, columns(me)], s_out.at[rank], r_out.at[rank], member(i)
            )
            back.start()
            pending.append(back)
    for rank in range(1, heads):
        source = slot(rank, -1)
        remote(
            acc.at[source],
            out_ref.at[:, columns(source)],
            s_out.at[rank],
            r_out.at[rank],
            member(source),
        ).wait_recv()
    for copy in pending:
        copy.wait_send()


def on_device(n_grp, n_seq, queries, keys, values, forget, beta, level_weights):
    size = queries.shape[0]
    heads = forget.shape[1]
    dim = queries.shape[1] // heads
    levels = level_weights.shape[0]
    bits = group_bits(heads, n_seq)
    total_bits = (n_grp * n_seq).bit_length() - 1
    low_levels, cross = len(bits) - 1, bits[-1]
    n_mid, n_up = cross - low_levels, total_bits - cross - 1
    decays = jnp.exp(-jnp.cumsum(forget, 0)).T
    small = jnp.concatenate(
        [
            decays[:, None],
            beta.T[:, None],
            jnp.transpose(level_weights, (2, 0, 1)),
            jnp.zeros((heads, AUX - 2 - levels, size), F32),
        ],
        1,
    )
    mids = [pltpu.VMEM((2, 2 * dim, dim), F32)] * n_mid
    ups = [pltpu.VMEM((2 * dim, dim), F32)] * (n_up - 1) + [pltpu.VMEM((dim, dim), F32)]
    dma = pltpu.SemaphoreType.DMA
    return pl.pallas_call(
        functools.partial(kernel, n_grp, n_seq, heads),
        out_shape=jax.ShapeDtypeStruct((size, heads * dim), F32),
        in_specs=[pl.BlockSpec(memory_space=pltpu.VMEM)] * 4,
        out_specs=pl.BlockSpec(memory_space=pltpu.VMEM),
        scratch_shapes=[
            pltpu.VMEM((heads, 2 * size + AUX, dim), F32),
            pltpu.VMEM((heads, size, dim), F32),
            pltpu.VMEM((heads, 2 * size + AUX, dim), F32),
            pltpu.VMEM((heads, size, dim), F32),
            pltpu.VMEM((heads, size, 2 * dim), F32),
            pltpu.VMEM((heads, size, AUX), F32),
            pltpu.VMEM((heads, 8, size), F32),
            pltpu.VMEM((heads, size, dim), F32),
            pltpu.VMEM((heads, size, dim), F32),
            pltpu.VMEM((2, 2 * dim, dim), F32),
        ]
        + [pltpu.VMEM((heads >> m, 2 * dim, dim), F32) for m in range(low_levels)]
        + mids
        + mids
        + ups
        + ups
        + [dma((heads,))] * 4
        + [dma((n_mid, 2))] * 2
        + [dma((n_up,))] * 2
        + [dma((heads,))] * 2,
        compiler_params=pltpu.CompilerParams(collective_id=0, has_side_effects=True),
    )(queries, keys, values, small)


def solution(mesh):
    both = P(("grp", "seq"), None)
    return jax.shard_map(
        functools.partial(on_device, mesh.shape["grp"], mesh.shape["seq"]),
        mesh=mesh,
        in_specs=(both, both, both, both, both, P(None, ("grp", "seq"), None)),
        out_specs=both,
        check_vma=False,
    )
```

time: 232 us -> 50.9 us (0.22)
  other arithmetic: 82 us -> 0.88 us
  waiting for transfers between devices: 63.6 us -> 0 us
  matrix products: 50.8 us -> 0 us
  Pallas kernels: 0 us -> 45.6 us
  local copies, waits for them, and re-layouts: 22.2 us -> 4.11 us
  starting transfers between devices: 11.8 us -> 0 us
    another operation x6 -> x1, other arithmetic: 79.5 us -> 0.17 us  [on_device(): decays = jnp.exp(-jnp.cumsum(forget, 0)).T]
    ppermute x9 -> x0, waiting for transfers between devices: 63.6 us -> none  [partner(): return lax.ppermute(block, axis, route)]
    dot_general x34 -> x0, matrix products: 48.7 us -> none  [the longest x26 32.3 us: contract(): return jnp.einsum(form, left, right, precision=lax.Precision.HIGHEST)]
    pallas_call x0 -> x1, Pallas kernels: none -> 45.6 us  [on_device(): pl.pallas_call(functools.partial(kernel, n_grp, n_seq, heads), out_shape=...]
    ppermute x9 -> x0, starting transfers between devices: 11.8 us -> none  [partner(): return lax.ppermute(block, axis, route)]
    mul x25 -> x0, local copies, waits for them, and re-layouts: 7.68 us -> none  [the longest x24 7.67 us: per_head(): weight_head[:, :, None] * reach_head[:, None, :]]
    unnamed x29 -> x9, local copies, waits for them, and re-layouts: 9.05 us -> 3.99 us
    another operation x6 -> x1, local copies, waits for them, and re-layouts: 3.96 us -> 0.05 us  [on_device(): decays = jnp.exp(-jnp.cumsum(forget, 0)).T]
  transfers between devices with their start and end apart: 9 -> 0, of which waited for: 5 -> 0; matrix products, arithmetic and copies ran while one was open for 12% -> 0% of each run, Pallas kernels for 0% -> 0%
where the time goes in v1:
time: 50.9 us; the launch traced here: 50.6 us
  Pallas kernels  45.6 us (90%)
  local copies, waits for them, and re-layouts  4.11 us (8%)
  other arithmetic  0.88 us (2%)
    pallas_call x1, Pallas kernels, on_device(): pl.pallas_call(functools.partial(kernel, n_grp, n_seq, heads), out_shape=...  45.6 us
    unnamed x9, local copies, waits for them, and re-layouts  3.99 us

profile of v1, /device:TPU:0, one launch (start us, length us, event | category | flops | bytes accessed | tf_op | source)
XLA Modules:
  0.0 50.6 jit_solution(16051170448994132997)
XLA Ops:
  0.0 0.0 copy-start.1
  0.0 0.1 pad.3.clone
  0.1 0.6 %copy-done.1 = f32[128,8]{0,1:T(8,128)S(1)} copy-done((f32[128,8]{0,1:T(8,128)S(1)}, f32[128,8]{0,1:T(8,128)}, u32[]{:S(2)}) %copy-start.1) | copy-done | bytes 4120
  0.7 0.1 copy.7
  0.8 0.2 reduce_window_sum.11
  1.0 0.0 copy-start
  1.0 0.7 %copy-done = f32[9,128,8]{1,2,0:T(8,128)S(1)} copy-done((f32[9,128,8]{1,2,0:T(8,128)S(1)}, f32[9,128,8]{1,2,0:T(8,128)}, u32[]{:S(2)}) %copy-start) | copy-done | bytes 36888
  1.7 0.0 copy-start.2
  1.7 0.7 %copy-done.2 = f32[128,8]{0,1:T(8,128)S(1)} copy-done((f32[128,8]{0,1:T(8,128)S(1)}, f32[128,8]{0,1:T(8,128)}, u32[]{:S(2)}) %copy-start.2) | copy-done | bytes 4120
  2.4 0.7 %maximum_maximum_fusion.refs_3_ = f32[8,16,128]{2,1,0:T(8,128)} fusion(f32[8,9,128]{2,1,0:T(8,128)S(1)} %bitcast.9, f32[8,1,128]{2,1,0:T(1,128)S(1)} %bitcast.11, f32[8,1,128]{2,1,0:T(1,128)S(1)} %bitcast.10, f32[16]{0:T(128)S(1)} %pad.3.clone), kind=kLoop, calls=%fused_computation | loop fusion | flops 49152 | bytes 110656 | tf_op jit(solution)/shard_map/concatenate | solution.py:339
  3.1 45.6 %shard_map.64 = f32[128,1024]{1,0:T(8,128)} custom-call(bf16[128,1024]{1,0:T(8,128)(2,1)} %refs_0_.1, bf16[128,1024]{1,0:T(8,128)(2,1)} %refs_1_.1, bf16[128,1024]{1,0:T(8,128)(2,1)} %refs_2_.1, f32[8,16,128]{2,1,0:T(8,128)} %maximum_maximum_fusion.refs_3_), custom_call_target="tpu_custom_call" | custom-call | tf_op jit(solution)/shard_map/pallas_call | solution.py:351
  48.7 1.9 %copy.13 = f32[128,1024]{1,0:T(8,128)} copy(f32[128,1024]{1,0:T(8,128)} %shard_map.64) | data formatting | bytes 1048576
  (4 shorter events, 0.1 us)
Async XLA Ops:
  0.0 0.7 %copy-start.1 = (f32[128,8]{0,1:T(8,128)S(1)}, f32[128,8]{0,1:T(8,128)}, u32[]{:S(2)}) copy-start(f32[128,8]{0,1:T(8,128)} %param.9) | copy-start | bytes 12292
  1.0 0.8 %copy-start = (f32[9,128,8]{1,2,0:T(8,128)S(1)}, f32[9,128,8]{1,2,0:T(8,128)}, u32[]{:S(2)}) copy-start(f32[9,128,8]{1,2,0:T(8,128)} %param.11) | copy-start | bytes 110596
  1.7 0.7 %copy-start.2 = (f32[128,8]{0,1:T(8,128)S(1)}, f32[128,8]{0,1:T(8,128)}, u32[]{:S(2)}) copy-start(f32[128,8]{0,1:T(8,128)} %param.10) | copy-start | bytes 12292

commit v2 on v1

--- a/solution.py
+++ b/solution.py
@@ -173,17 +173,26 @@
         return copy
 
     pending = []
-    kv_copies, q_copies = [], []
+    kv_copies, q_copies = {}, {}
     for out, into, send, receive, copies in (
         (kv_out, kv_in, s_kv, r_kv, kv_copies),
         (q_out, q_in, s_q, r_q, q_copies),
     ):
         for rank in range(1, heads):
             i = slot(rank, 1)
-            copy = remote(out.at[i], into.at[me], send.at[rank], receive.at[rank], member(i))
-            copy.start()
-            copies.append(copy)
-    pending += kv_copies + q_copies
+            copies[rank] = remote(
+                out.at[i], into.at[me], send.at[rank], receive.at[rank], member(i)
+            )
+    for copy in kv_copies.values():
+        copy.start()
+    pending += list(kv_copies.values()) + list(q_copies.values())
+
+    def send_queries(ranks):
+        for rank in ranks:
+            if 0 < rank < heads:
+                q_copies[rank].start()
+
+    send_queries((1, half, half + 1))
     kv_in[me] = kv_out[me]
     q_in[me] = q_out[me]
 
@@ -208,7 +217,7 @@
             slots = []
             for rank in (far * half + first, far * half + first + 1):
                 if rank:
-                    kv_copies[rank - 1].wait_recv()
+                    kv_copies[rank].wait_recv()
                 slots.append(slot(rank, -1))
             done = transitions([kv_in[i] for i in slots], size, dim)
             for i, (node, pair, col, rk_row) in zip(slots, done):
@@ -227,6 +236,7 @@
                 else:
                     mid_out[0][which] = node
         first_mid.append(send_mid(0, which))
+        send_queries(range(far * half + 2, far * half + half))
 
     def read(j, lower, l, gate=None):
         seen = mm(split(reach[j]), lower, NT)
@@ -239,7 +249,7 @@
     for first in range(0, heads, 2):
         for rank in (first, first + 1):
             if rank:
-                q_copies[rank - 1].wait_recv()
+                q_copies[rank].wait_recv()
             i = slot(rank, -1)
             rk_row = jnp.broadcast_to(rks[i][:1], (size, size))
             near = local_reads(
@@ -350,7 +360,7 @@
     dma = pltpu.SemaphoreType.DMA
     return pl.pallas_call(
         functools.partial(kernel, n_grp, n_seq, heads),
-        out_shape=jax.ShapeDtypeStruct((size, heads * dim), F32),
+        out_shape=pltpu.VMEM((size, heads * dim), F32),
         in_specs=[pl.BlockSpec(memory_space=pltpu.VMEM)] * 4,
         out_specs=pl.BlockSpec(memory_space=pltpu.VMEM),
         scratch_shapes=[

time: 50.9 us -> 48.2 us (0.947)
  Pallas kernels: 45.6 us -> 44 us
  local copies, waits for them, and re-layouts: 4.11 us -> 3.02 us
    pallas_call x1, Pallas kernels: 45.6 us -> 44 us  [on_device(): pl.pallas_call(functools.partial(kernel, n_grp, n_seq, heads), out_shape=...]
    unnamed x9, local copies, waits for them, and re-layouts: 3.99 us -> 2.9 us
where the time goes in v2:
time: 48.2 us; the launch traced here: 47.9 us
  Pallas kernels  44 us (91%)
  local copies, waits for them, and re-layouts  3.02 us (6%)
  other arithmetic  0.88 us (2%)
    pallas_call x1, Pallas kernels, on_device(): pl.pallas_call(functools.partial(kernel, n_grp, n_seq, heads), out_shape=...  44 us
    unnamed x9, local copies, waits for them, and re-layouts  2.9 us

profile of v2, /device:TPU:0, one launch (start us, length us, event | category | flops | bytes accessed | tf_op | source)
XLA Modules:
  0.0 47.9 jit_solution(18281852953725418736)
XLA Ops:
  0.0 0.0 copy-start.1
  0.0 0.1 pad.3.clone
  0.1 0.6 %copy-done.1 = f32[128,8]{0,1:T(8,128)S(1)} copy-done((f32[128,8]{0,1:T(8,128)S(1)}, f32[128,8]{0,1:T(8,128)}, u32[]{:S(2)}) %copy-start.1) | copy-done | bytes 4120
  0.7 0.1 copy.7
  0.8 0.2 reduce_window_sum.11
  1.0 0.0 copy-start
  1.0 0.7 %copy-done = f32[9,128,8]{1,2,0:T(8,128)S(1)} copy-done((f32[9,128,8]{1,2,0:T(8,128)S(1)}, f32[9,128,8]{1,2,0:T(8,128)}, u32[]{:S(2)}) %copy-start) | copy-done | bytes 36888
  1.7 0.0 copy-start.2
  1.7 0.7 %copy-done.2 = f32[128,8]{0,1:T(8,128)S(1)} copy-done((f32[128,8]{0,1:T(8,128)S(1)}, f32[128,8]{0,1:T(8,128)}, u32[]{:S(2)}) %copy-start.2) | copy-done | bytes 4120
  2.4 0.7 %maximum_maximum_fusion.refs_3_ = f32[8,16,128]{2,1,0:T(8,128)} fusion(f32[8,9,128]{2,1,0:T(8,128)S(1)} %bitcast.9, f32[8,1,128]{2,1,0:T(1,128)S(1)} %bitcast.11, f32[8,1,128]{2,1,0:T(1,128)S(1)} %bitcast.10, f32[16]{0:T(128)S(1)} %pad.3.clone), kind=kLoop, calls=%fused_computation | loop fusion | flops 49152 | bytes 110656 | tf_op jit(solution)/shard_map/concatenate | solution.py:349
  3.1 44.0 %shard_map.64 = f32[128,1024]{1,0:T(8,128)S(1)} custom-call(bf16[128,1024]{1,0:T(8,128)(2,1)} %refs_0_.1, bf16[128,1024]{1,0:T(8,128)(2,1)} %refs_1_.1, bf16[128,1024]{1,0:T(8,128)(2,1)} %refs_2_.1, f32[8,16,128]{2,1,0:T(8,128)} %maximum_maximum_fusion.refs_3_), custom_call_target="tpu_custom_call" | custom-call | tf_op jit(solution)/shard_map/pallas_call | solution.py:361
  47.1 0.8 %copy.13 = f32[128,1024]{1,0:T(8,128)} copy(f32[128,1024]{1,0:T(8,128)S(1)} %shard_map.64) | data formatting | bytes 1048576
  (4 shorter events, 0.1 us)
Async XLA Ops:
  0.0 0.7 %copy-start.1 = (f32[128,8]{0,1:T(8,128)S(1)}, f32[128,8]{0,1:T(8,128)}, u32[]{:S(2)}) copy-start(f32[128,8]{0,1:T(8,128)} %param.9) | copy-start | bytes 12292
  1.0 0.8 %copy-start = (f32[9,128,8]{1,2,0:T(8,128)S(1)}, f32[9,128,8]{1,2,0:T(8,128)}, u32[]{:S(2)}) copy-start(f32[9,128,8]{1,2,0:T(8,128)} %param.11) | copy-start | bytes 110596
  1.7 0.7 %copy-start.2 = (f32[128,8]{0,1:T(8,128)S(1)}, f32[128,8]{0,1:T(8,128)}, u32[]{:S(2)}) copy-start(f32[128,8]{0,1:T(8,128)} %param.10) | copy-start | bytes 12292
